TPU v7x, 32 devices: a whole 2x2x4 slice. The times are simulated.
32 devices in a mesh: prow: 8 (over z, x), pcol: 4 (over y, core).
Axes of the slice: x: 2, y: 2, z: 4, core: 2. Of those that a mesh axis runs over, the one named last changes fastest.
Arguments:
- eigvecs: float32 [16384, 2048], P('prow', 'pcol'), may hold values from -6 to 6
- reflectors: float32 [4, 16384, 256], P(None, 'prow'), may hold values from -0.046875 to 0.046875
- triangles: float32 [4, 256, 256], replicated, may hold values from -1 to 2, as said below
Outputs:
- transformed: float32 [16384, 2048], P('prow', 'pcol')
Inputs may be any that keep to these rules, and one draw needn't show every extreme that they name: Each triangles[k] is upper triangular with diagonal entries between 1 and 2.
All inputs are finite; a program needn't handle non-finite values.
Results may differ from a plain program's by a relative error of at most 0.0001.
Values sent between devices are 32-bit elements; how exact they have to be, the bound alone decides.
No kernel may reach another device: no remote copies, remote signals or barrier semaphores. Data moves between devices by JAX's collectives and lax.ppermute only.
A program may use at most 128 MiB of HBM per device.

v0:
```python
import functools

import jax
import jax.numpy as jnp
from jax import lax
from jax.experimental import pallas as pl
from jax.experimental.pallas import tpu as pltpu
from jax.sharding import PartitionSpec as P


RB = 64
TILES = 8


def split(value):
    high = value.astype(jnp.bfloat16)
    return high, (value - high.astype(jnp.float32)).astype(jnp.bfloat16)


def dot3(left, right, dims=(1, 0)):
    def one(a, b):
        return lax.dot_general(a, b, ((dims[:1], dims[1:]), ((), ())), preferred_element_type=jnp.float32)

    return one(left[0], right[0]) + (one(left[0], right[1]) + one(left[1], right[0]))


def unit(raw, panel, first_row, owner, size):
    _, width = raw.shape
    local = first_row + lax.broadcasted_iota(jnp.int32, raw.shape, 0)
    grow = ((local // RB) * size + owner) * RB + local % RB
    column = panel * width + lax.broadcasted_iota(jnp.int32, raw.shape, 1)
    return jnp.where(grow < column, 0.0, jnp.where(grow == column, 1.0, raw))


def rows_of(tile, rows):
    return slice(tile * (rows // TILES), (tile + 1) * (rows // TILES))


def covered_rows(panels, width, size):
    return RB * -(-panels * width // (RB * size))


def load_split(raw, panel, rows, total_panels, owner, size):
    if rows.start < covered_rows(total_panels, raw.shape[1], size):
        raw = unit(raw, panel, rows.start, owner, size)
    return split(raw)


def emit(total, order, kk_ref, ks_ref, s_ref):
    rows = kk_ref.shape[0]
    for at, ref in enumerate((kk_ref, ks_ref, s_ref.at[0], s_ref.at[1])):
        start = pl.multiple_of((order ^ at) * rows, 8)
        ref[...] = total[pl.ds(start, rows), :]


def late_order(panel, scal):
    return scal[1 + panel % 2]


def first_kernel(size, scal, w_hbm, v_hbm, kk_ref, ks_ref, s_ref, wh, wl, eh, el, lh, ll, wbuf, vbuf, total, sem):
    panels, rows, width = vbuf.shape
    count = eh.shape[1] // width

    def fetch(k, t):
        r = rows_of(t, rows)
        if k < 0:
            return pltpu.make_async_copy(w_hbm.at[r], wbuf.at[r], sem.at[panels, t])
        return pltpu.make_async_copy(v_hbm.at[k, r], vbuf.at[k, r], sem.at[k, t])

    early = [[fetch(k, t) for k in range(-1, count)] for t in range(TILES)]
    late = [[fetch(k, t) for k in range(count, panels)] for t in range(TILES)]
    for copies in early + late:
        for copy in copies:
            copy.start()
    for t in range(TILES):
        r = rows_of(t, rows)
        for copy in early[t]:
            copy.wait()
        left = split(wbuf[r, :].T)
        wh[:, r], wl[:, r] = left
        for k in range(count):
            right = load_split(vbuf[k, r, :], k, r, panels, scal[0], size)
            c = slice(k * width, (k + 1) * width)
            eh[r, c], el[r, c] = right
            value = dot3(left, right)
            total[k] = value if t == 0 else total[k] + value
    for k in range(count):
        emit(total.at[k], scal[2], kk_ref.at[k], ks_ref.at[k], s_ref.at[k])
    for t in range(TILES):
        r = rows_of(t, rows)
        for copy in late[t]:
            copy.wait()
        for k in range(count, panels):
            c = slice((k - count) * width, (k - count + 1) * width)
            lh[r, c], ll[r, c] = load_split(vbuf[k, r, :], k, r, panels, scal[0], size)


def second_kernel(scal, wh, wl, vh, vl, *refs):
    for k in range(len(refs) // 3):
        kk_ref, ks_ref, s_ref = refs[3 * k : 3 * k + 3]
        rows, width = kk_ref.shape
        c = slice(k * width, (k + 1) * width)
        at = [pl.ds(pl.multiple_of((late_order(k, scal) ^ b) * rows, rows), rows) for b in range(4)]
        left = [jnp.concatenate([ref[b, :] for b in at], 0) for ref in (wh, wl)]
        value = dot3(left, (vh[:, c], vl[:, c]))
        kk_ref[...], ks_ref[...] = value[:rows], value[rows : 2 * rows]
        s_ref[0], s_ref[1] = value[2 * rows : 3 * rows], value[3 * rows :]


def pairs_kernel(count, scal, eh, el, lh, ll, kk_ref, ks_ref, s_ref, total):
    half = total.shape[1]
    panels = 2 * count

    def columns(k, which):
        return pl.ds(pl.multiple_of((2 * (k % count) + which) * half, half), half)

    def side(chosen, which):
        highs = [(eh if k < count else lh)[:, columns(k, which)] for k in chosen]
        lows = [(el if k < count else ll)[:, columns(k, which)] for k in chosen]
        return jnp.concatenate(highs, 1), jnp.concatenate(lows, 1)

    for top in range(panels - 1, 0, -2):
        right_panels = [k for k in (top - 1, top) if k > 0]
        value = dot3(side(range(top), scal[4]), side(right_panels, scal[3]), (0, 0))
        for at, k in enumerate(right_panels):
            for j in range(k):
                to = slice(pair_index(j, k) * half, (pair_index(j, k) + 1) * half)
                total[to, :] = value[j * half : (j + 1) * half, at * half : (at + 1) * half]
    emit(total, scal[1], kk_ref, ks_ref, s_ref)


def pair_index(j, k):
    return k * (k - 1) // 2 + j


def place(blocks, order, out):
    rows = blocks[0].shape[0]
    for at, ref in enumerate(blocks):
        out[pl.ds(pl.multiple_of((order ^ at) * rows, 8), rows), :] = ref[...]


def place_parts(scal, quarters, parts):
    rows = parts.shape[2] // 4
    for at, ref in enumerate(quarters):
        place([ref.at[pl.ds(b * rows, rows)] for b in range(4)], scal[1], parts.at[scal[3] ^ (at & 1), scal[4] ^ (at >> 1)])


def pair(parts, j, k):
    half = parts.shape[3]
    at = slice(pair_index(j, k) * half, (pair_index(j, k) + 1) * half)
    return jnp.concatenate([jnp.concatenate([parts[0, b, at, :], parts[1, b, at, :]], 1) for b in range(2)], 0)


def subtract(value, vh, vl, r, coeff):
    return value - dot3((vh[r, :], vl[r, :]), coeff)


def blocks_at(panel, turned, mine, near0, near1, far):
    inner, outer = (near0, near1) if turned else (near1, near0)
    return [ref.at[panel] for ref in (mine, inner, outer, far)]


def fold_kernel(count, scal, q0, q1, q2, q3, tri, vh, vl, uh, ul, ph, plow, rh, rl, parts):
    width = tri.shape[2]
    place_parts(scal, (q0, q1, q2, q3), parts)
    ph[...], plow[...] = split(pair(parts, 0, 1))
    for j in range(count):
        for k in range(count):
            to = (slice(j * width, (j + 1) * width), slice(k * width, (k + 1) * width))
            rh[to], rl[to] = split(pair(parts, j, count + k))
    first, second = split(tri[0]), split(tri[1])
    cross = dot3(second, split(pair(parts, count, count + 1)), (1, 1))
    cross = dot3(split(cross), first)
    mixed = split(jnp.concatenate([tri[0], -cross], 0))
    for t in range(TILES):
        r = rows_of(t, vh.shape[0])
        uh[r, :width], ul[r, :width] = split(dot3((vh[r, :], vl[r, :]), mixed))
        uh[r, width:], ul[r, width:] = split(dot3((vh[r, width:], vl[r, width:]), second))


def middle_kernel(scal, mine, near0, near1, far, tri, ph, plow, rh, rl, w_ref, vh, vl, o_ref, pre, proj):
    for k in range(2):
        place(blocks_at(k, True, mine, near0, near1, far), scal[2], proj.at[k])
    first = dot3(split(proj[0]), split(tri[0]), (1, 1))
    second = proj[1] - dot3(split(first), (ph[...], plow[...]))
    second = dot3(split(second), split(tri[1]), (1, 1))
    coeff = jnp.concatenate([first, second], 1)
    turned = split(coeff.T)
    pre[...] = dot3(split(coeff), (rh[...], rl[...]))
    for t in range(TILES):
        r = rows_of(t, w_ref.shape[0])
        o_ref[r, :] = subtract(w_ref[r, :], vh, vl, r, turned)


def last_kernel(scal, mine, near0, near1, far, pre, w_ref, uh, ul, o_hbm, proj, obuf, sem):
    count, _, _ = proj.shape
    for k in range(count):
        place(blocks_at(k, k % 2 == 1, mine, near0, near1, far), late_order(k, scal), proj.at[k])
    turned = split((jnp.concatenate([proj[k] for k in range(count)], 1) - pre[...]).T)
    copies = []
    steps = sem.shape[0]
    for t in range(steps):
        tall = w_ref.shape[0] // steps
        r = slice(t * tall, (t + 1) * tall)
        obuf[r, :] = subtract(w_ref[r, :], uh, ul, r, turned)
        copies.append(pltpu.make_async_copy(obuf.at[r], o_hbm.at[r], sem.at[t]))
        copies[-1].start()
    for copy in copies:
        copy.wait()


CHIP = pl.BlockSpec(memory_space=pltpu.VMEM)
FAR = pl.BlockSpec(memory_space=pltpu.HBM)


def call(kernel, args, in_specs, outs, out_specs, scratch, flops, limit):
    return pl.pallas_call(
        kernel,
        in_specs=[pl.BlockSpec(memory_space=pltpu.SMEM)] + in_specs,
        out_specs=out_specs,
        out_shape=outs,
        scratch_shapes=scratch,
        compiler_params=pltpu.CompilerParams(vmem_limit_bytes=limit << 20),
        cost_estimate=pl.CostEstimate(flops=flops, bytes_accessed=0, transcendentals=0),
    )(*args)


def far(value):
    return pltpu.with_memory_space_constraint(value, pltpu.HBM)


def shape(*dims, dtype=jnp.float32):
    return jax.ShapeDtypeStruct(dims, dtype)


def blocks_of(tall, wide, *lead):
    return [shape(*lead, tall // 4, wide), shape(*lead, tall // 4, wide), shape(*lead, 2, tall // 4, wide)]


def pair_of(*dims):
    return [shape(*dims, dtype=jnp.bfloat16)] * 2


def project_first(scal, eigvecs, reflectors, count):
    rows, cols = eigvecs.shape
    panels, _, width = reflectors.shape
    out = call(
        functools.partial(first_kernel, lax.axis_size("prow")),
        (scal, far(eigvecs), far(reflectors)),
        [FAR, FAR],
        blocks_of(cols, width, count) + pair_of(cols, rows) + pair_of(rows, count * width) + pair_of(rows, (panels - count) * width),
        [CHIP] * 9,
        [
            pltpu.VMEM((rows, cols), jnp.float32),
            pltpu.VMEM((panels, rows, width), jnp.float32),
            pltpu.VMEM((count, cols, width), jnp.float32),
            pltpu.SemaphoreType.DMA((panels + 1, TILES)),
        ],
        6 * rows * cols * count * width,
        24,
    )
    return out[:3], out[3:5], out[5:7], out[7:]


def pair_products(scal, early, late, width):
    rows, wide = early[0].shape
    count = wide // width
    half = width // 2
    tall = count * (2 * count - 1) * half
    return call(
        functools.partial(pairs_kernel, count),
        (scal, *early, *late),
        [CHIP] * 4,
        blocks_of(tall, half),
        [CHIP] * 3,
        [pltpu.VMEM((tall, half), jnp.float32)],
        6 * rows * tall * half,
        16,
    )


def project_second(scal, turned, late, width):
    cols, rows = turned[0].shape
    count = late[0].shape[1] // width
    out = call(
        second_kernel,
        (scal, *turned, *late),
        [CHIP] * 4,
        blocks_of(cols, width) * count,
        [CHIP] * (3 * count),
        [],
        6 * rows * cols * count * width,
        12,
    )
    return [out[3 * k : 3 * k + 3] for k in range(count)]


def fold(scal, quarters, tri, late):
    rows, wide = late[0].shape
    count, width, _ = tri.shape
    out = call(
        functools.partial(fold_kernel, count),
        (scal, *quarters, tri, *late),
        [CHIP] * 7,
        pair_of(rows, wide) + pair_of(width, width) + pair_of(wide, wide),
        [CHIP] * 6,
        [pltpu.VMEM((2, 2) + quarters[0].shape, jnp.float32)],
        6 * rows * width * width * 3,
        12,
    )
    return out[:2], out[2:]


def update_middle(scal, blocks, tri, joined, work, early):
    rows, cols = work.shape
    count, width, _ = tri.shape
    return call(
        middle_kernel,
        (scal, *blocks, tri, *joined, work, *early),
        [CHIP] * 12,
        [shape(rows, cols), shape(cols, count * width)],
        [CHIP] * 2,
        [pltpu.VMEM((count, cols, width), jnp.float32)],
        6 * rows * cols * count * width,
        12,
    )


def update_last(scal, blocks, pre, work, folded):
    rows, cols = work.shape
    count, width = blocks[0].shape[0], blocks[0].shape[2]
    return call(
        last_kernel,
        (scal, *blocks, pre, work, *folded),
        [CHIP] * 8,
        shape(rows, cols),
        FAR,
        [pltpu.VMEM((count, cols, width), jnp.float32), pltpu.VMEM((rows, cols), jnp.float32), pltpu.SemaphoreType.DMA((2 * TILES,))],
        6 * rows * cols * count * width,
        16,
    )


def bit_of(axis, bit):
    return (lax.axis_index(axis) >> bit) & 1


def swap(value, axis, flip):
    size = lax.axis_size(axis)
    return lax.ppermute(value, axis, [(i, i ^ flip) for i in range(size)])


def reduced(parts, outer, inner):
    keep_keep, keep_send, send = parts
    got = swap(send, "prow", outer)
    passed = keep_send + got[..., 1, :, :]
    return keep_keep, got[..., 0, :, :], swap(passed, "prow", inner)


def rest_summed(value):
    flip = 4
    while flip < lax.axis_size("prow"):
        got = swap(value, "prow", flip)
        value = value + got
        flip *= 2
    return value


def one_reduced(parts, outer, inner):
    a, b, c = reduced(parts, outer, inner)
    value = a + b + c
    return rest_summed(value)


def two_reduced(even, odd):
    even, odd = reduced(even, 1, 2), reduced(odd, 2, 1)
    value = jnp.stack([a + b + c for a, b, c in (even, odd)])
    return rest_summed(value)


def shared(value):
    return swap(value, "prow", 1), swap(value, "prow", 2)


def body(eigvecs, reflectors, triangles):
    panels, _, width = reflectors.shape
    count = panels // 2
    low, high = bit_of("prow", 0), bit_of("prow", 1)
    scal = jnp.stack([lax.axis_index("prow"), low * 2 + high, high * 2 + low, bit_of("pcol", 1), bit_of("pcol", 0)]).astype(jnp.int32)

    first, turned, early, late = project_first(scal, eigvecs, reflectors, count)
    pairs = pair_products(scal, early, late, width)
    second = project_second(scal, turned, late, width)
    pairs = one_reduced(pairs, 1, 2)
    near0, near1 = shared(pairs)
    diag = swap(pairs, "prow", 3)
    pairs = jnp.concatenate([pairs, near1, near0, diag], 0)
    across = swap(pairs, "pcol", 2)
    quarters = (pairs, across, swap(pairs, "pcol", 1), swap(across, "pcol", 1))
    mine = one_reduced(first, 2, 1)
    near0, near1 = shared(mine)
    folded, joined = fold(scal, quarters, triangles[count:], late)
    blocks = (mine, near0, near1, swap(mine, "prow", 3))
    work, pre = update_middle(scal, blocks, triangles[:count], joined, eigvecs, early)
    mine = two_reduced(*second)
    return update_last(scal, (mine, *shared(mine), swap(mine, "prow", 3)), pre, work, folded)


def solution(mesh):
    in_specs = (P("prow", "pcol"), P(None, "prow", None), P())
    out_specs = P("prow", "pcol")
    return jax.shard_map(body, mesh=mesh, in_specs=in_specs, out_specs=out_specs, check_vma=False)
```

profile of v0, /device:TPU:0, one launch (start us, length us, event | category | flops | bytes accessed | tf_op | source)
XLA Modules:
  0.0 108.1 jit_solution(16686225761674203755)
XLA Ops:
  0.0 0.1 stack.32.scal
  0.1 7.4 %shard_map.37 = (f32[2,128,256]{2,1,0:T(8,128)S(1)}, f32[2,128,256]{2,1,0:T(8,128)S(1)}, f32[2,2,128,256]{3,2,1,0:T(8,128)S(1)}, bf16[512,2048]{1,0:T(8,128)(2,1...) custom-call(s32[5]{0:T(128)S(1)} %stack.32.scal, ...), custom_call_target="tpu_custom_call" | custom-call | flops 3221225472 | tf_op jit(solution)/shard_map/pallas_call | solution.py:217
  7.5 2.4 %shard_map.39 = (f32[192,128]{1,0:T(8,128)S(1)}, f32[192,128]{1,0:T(8,128)S(1)}, f32[2,192,128]{2,1,0:T(8,128)S(1)}) custom-call(s32[5]{0:T(128)S(1)} %stack.32.scal, bf16[2048,512]{1,0:T(8,128)(2,1)S(1)} %get-tuple-element.44.eh.vh, bf16[2048,512]{1,0:T(8,128)(2,1)S(1)} %get-tuple-element.45.el.vl, bf16[2048,512]{1,0:T(8,128)(2,1)S(1)} %get-tuple-element.33.vh.lh, ...), custom_call_target="tpu_custom_call" | custom-call | flops 1207959552 | tf_op jit(solution)/shard_map/pallas_call | solution.py:217
  9.9 3.0 %collective-permute-start.14 = (f32[2,192,128]{2,1,0:T(8,128)S(1)}, f32[2,192,128]{2,1,0:T(8,128)S(1)}, u32[]{:S(2)}, u32[]{:S(2)}) collective-permute-start(f32[2,192,128]{2,1,0:T(8,128)S(1)} %get-tuple-element.47), channel_id=1, source_target_pairs={{0,4},{4,0},{8,12},{12,8},{16,20},{20,16},{24,28},{28,24},{1,5},{5... | collective-permute-start | bytes 589832 | tf_op jit(solution)/shard_map/ppermute | solution.py:350
  12.9 3.9 %shard_map.38 = (f32[128,256]{1,0:T(8,128)S(1)}, f32[128,256]{1,0:T(8,128)S(1)}, f32[2,128,256]{2,1,0:T(8,128)S(1)}, f32[128,256]{1,0:T(8,128)S(1)}, f32[128,256]{1,0:T(8,128)S(1)}, /*index=5*/f32[2,128,256]{2,1,0:T(8,128)S(1)}) custom-call(s32[5]{0:T(128)S(1)} %stack.32.scal, bf16[512,2048]{1,0:T(8,128)(2,1)S(1)} %get-tuple-element.31.wh, ...), custom_call_target="tpu_custom_call" | custom-call | flops 3221225472 | tf_op jit(solution)/shard_map/pallas_call | solution.py:217
  16.9 0.1 collective-permute-start
  17.0 2.1 %collective-permute-start.2 = (f32[2,128,256]{2,1,0:T(8,128)S(1)}, f32[2,128,256]{2,1,0:T(8,128)S(1)}, u32[]{:S(2)}, u32[]{:S(2)}) collective-permute-start(f32[2,128,256]{2,1,0:T(8,128)S(1)} %get-tuple-element.39), channel_id=1, source_target_pairs={{0,8},{4,12},{8,0},{12,4},{16,24},{20,28},{24,16},{28,20},{1,9},{5... | collective-permute-start | bytes 786440 | tf_op jit(solution)/shard_map/ppermute | solution.py:350
  19.1 0.1 collective-permute-start.8
  19.2 0.0 collective-permute-done.14
  19.2 2.1 %collective-permute-start.15 = (f32[192,128]{1,0:T(8,128)S(1)}, f32[192,128]{1,0:T(8,128)S(1)}, u32[]{:S(2)}, u32[]{:S(2)}) collective-permute-start(f32[192,128]{1,0:T(8,128)S(1)} %fusion.11), channel_id=1, source_target_pairs={{0,8},{4,12},{8,0},{12,4},{16,24},{20,28},{24,16},{28,20},{1,9},{5... | collective-permute-start | bytes 294920 | tf_op jit(solution)/shard_map/ppermute | solution.py:350
  21.3 3.4 %collective-permute-done = f32[2,128,256]{2,1,0:T(8,128)S(1)} collective-permute-done((f32[2,128,256]{2,1,0:T(8,128)S(1)}, f32[2,128,256]{2,1,0:T(8,128)S(1)}, u32[]{:S(2)}, u32[]{:S(2)}) %collective-permute-start) | collective-permute-done | bytes 262176 | tf_op jit(solution)/shard_map/ppermute | solution.py:350
  24.7 1.6 %collective-permute-start.1 = (f32[128,256]{1,0:T(8,128)S(1)}, f32[128,256]{1,0:T(8,128)S(1)}, u32[]{:S(2)}, u32[]{:S(2)}) collective-permute-start(f32[128,256]{1,0:T(8,128)S(1)} %fusion.7), channel_id=1, source_target_pairs={{0,8},{4,12},{8,0},{12,4},{16,24},{20,28},{24,16},{28,20},{1,9},{5... | collective-permute-start | bytes 393224 | tf_op jit(solution)/shard_map/ppermute | solution.py:350
  26.4 13.2 %collective-permute-done.15 = f32[192,128]{1,0:T(8,128)S(1)} collective-permute-done((f32[192,128]{1,0:T(8,128)S(1)}, f32[192,128]{1,0:T(8,128)S(1)}, u32[]{:S(2)}, u32[]{:S(2)}) %collective-permute-start.15) | collective-permute-done | bytes 98336 | tf_op jit(solution)/shard_map/ppermute | solution.py:350
  39.6 3.1 %collective-permute-start.16 = (f32[192,128]{1,0:T(8,128)S(1)}, f32[192,128]{1,0:T(8,128)S(1)}, u32[]{:S(2)}, u32[]{:S(2)}) collective-permute-start(f32[192,128]{1,0:T(8,128)S(1)} %fusion.13), channel_id=1, source_target_pairs={{0,16},{4,20},{8,24},{12,28},{16,0},{20,4},{24,8},{28,12},{1,17},{... | collective-permute-start | bytes 294920 | tf_op jit(solution)/shard_map/ppermute | solution.py:350
  42.7 0.0 collective-permute-done.2
  42.7 1.5 %collective-permute-start.3 = (f32[128,256]{1,0:T(8,128)S(1)}, f32[128,256]{1,0:T(8,128)S(1)}, u32[]{:S(2)}, u32[]{:S(2)}) collective-permute-start(f32[128,256]{1,0:T(8,128)S(1)} %fusion.3), channel_id=1, source_target_pairs={{0,4},{4,0},{8,12},{12,8},{16,20},{20,16},{24,28},{28,24},{1,5},{5... | collective-permute-start | bytes 393224 | tf_op jit(solution)/shard_map/ppermute | solution.py:350
  44.2 1.1 collective-permute-done.16
  45.3 2.9 %collective-permute-start.19 = (f32[192,128]{1,0:T(8,128)S(1)}, f32[192,128]{1,0:T(8,128)S(1)}, u32[]{:S(2)}, u32[]{:S(2)}) collective-permute-start(f32[192,128]{1,0:T(8,128)S(1)} %add.67), channel_id=1, source_target_pairs={{0,12},{4,8},{8,4},{12,0},{16,28},{20,24},{24,20},{28,16},{1,13},{... | collective-permute-start | bytes 294920 | tf_op jit(solution)/shard_map/ppermute | solution.py:350
  48.2 0.5 collective-permute-start.18
  48.7 0.2 collective-permute-start.17
  48.9 2.0 %collective-permute-done.19 = f32[192,128]{1,0:T(8,128)S(1)} collective-permute-done((f32[192,128]{1,0:T(8,128)S(1)}, f32[192,128]{1,0:T(8,128)S(1)}, u32[]{:S(2)}, u32[]{:S(2)}) %collective-permute-start.19) | collective-permute-done | bytes 98336 | tf_op jit(solution)/shard_map/ppermute | solution.py:350
  50.9 1.9 %collective-permute-done.18 = f32[192,128]{1,0:T(8,128)S(1)} collective-permute-done((f32[192,128]{1,0:T(8,128)S(1)}, f32[192,128]{1,0:T(8,128)S(1)}, u32[]{:S(2)}, u32[]{:S(2)}) %collective-permute-start.18) | collective-permute-done | bytes 98336 | tf_op jit(solution)/shard_map/ppermute | solution.py:350
  52.8 0.5 collective-permute-done.17
  53.4 1.6 %collective-permute-start.20 = (f32[768,128]{1,0:T(8,128)S(1)}, f32[768,128]{1,0:T(8,128)S(1)}, u32[]{:S(2)}, u32[]{:S(2)}) collective-permute-start(f32[768,128]{1,0:T(8,128)S(1)} %pad_maximum_fusion.q0), channel_id=1, source_target_pairs={{0,2},{1,3},{2,0},{3,1},{4,6},{5,7},{6,4},{7,5},{8,10},{9,11},{10,... | collective-permute-start | bytes 1179656 | tf_op jit(solution)/shard_map/ppermute | solution.py:350
  55.0 1.6 %collective-permute-start.9 = (f32[2,128,256]{2,1,0:T(8,128)S(1)}, f32[2,128,256]{2,1,0:T(8,128)S(1)}, u32[]{:S(2)}, u32[]{:S(2)}) collective-permute-start(f32[2,128,256]{2,1,0:T(8,128)S(1)} %fusion), channel_id=1, source_target_pairs={{0,4},{4,0},{8,12},{12,8},{16,20},{20,16},{24,28},{28,24},{1,5},{5... | collective-permute-start | bytes 786440 | tf_op jit(solution)/shard_map/ppermute | solution.py:350
  56.5 0.0 collective-permute-done.3
  56.6 4.6 %collective-permute-start.4 = (f32[2,128,256]{2,1,0:T(8,128)S(1)}, f32[2,128,256]{2,1,0:T(8,128)S(1)}, u32[]{:S(2)}, u32[]{:S(2)}) collective-permute-start(f32[2,128,256]{2,1,0:T(8,128)S(1)} %pad_maximum_fusion.1), channel_id=1, source_target_pairs={{0,16},{4,20},{8,24},{12,28},{16,0},{20,4},{24,8},{28,12},{1,17},{... | collective-permute-start | bytes 786440 | tf_op jit(solution)/shard_map/ppermute | solution.py:350
  61.2 0.0 collective-permute-start.21
  61.2 0.2 collective-permute-done.9
  61.4 0.1 fusion.2
  61.5 4.6 %collective-permute-start.10 = (f32[2,128,256]{2,1,0:T(8,128)S(1)}, f32[2,128,256]{2,1,0:T(8,128)S(1)}, u32[]{:S(2)}, u32[]{:S(2)}) collective-permute-start(f32[2,128,256]{2,1,0:T(8,128)S(1)} %fusion.2), channel_id=1, source_target_pairs={{0,16},{4,20},{8,24},{12,28},{16,0},{20,4},{24,8},{28,12},{1,17},{... | collective-permute-start | bytes 786440 | tf_op jit(solution)/shard_map/ppermute | solution.py:350
  66.1 0.1 fusion.15
  66.2 12.4 %collective-permute-done.10 = f32[2,128,256]{2,1,0:T(8,128)S(1)} collective-permute-done((f32[2,128,256]{2,1,0:T(8,128)S(1)}, f32[2,128,256]{2,1,0:T(8,128)S(1)}, u32[]{:S(2)}, u32[]{:S(2)}) %collective-permute-start.10) | collective-permute-done | bytes 262176 | tf_op jit(solution)/shard_map/ppermute | solution.py:350
  78.6 1.0 collective-permute-start.13
  79.6 2.0 %collective-permute-start.12 = (f32[2,128,256]{2,1,0:T(8,128)S(1)}, f32[2,128,256]{2,1,0:T(8,128)S(1)}, u32[]{:S(2)}, u32[]{:S(2)}) collective-permute-start(f32[2,128,256]{2,1,0:T(8,128)S(1)} %add.63.mine), channel_id=1, source_target_pairs={{0,8},{4,12},{8,0},{12,4},{16,24},{20,28},{24,16},{28,20},{1,9},{5... | collective-permute-start | bytes 786440 | tf_op jit(solution)/shard_map/ppermute | solution.py:350
  81.6 0.0 collective-permute-done.4
  81.6 0.6 collective-permute-start.11
  82.2 0.0 collective-permute-done.21.q2
  82.2 1.0 collective-permute-start.7
  83.2 2.0 %collective-permute-start.6 = (f32[2,128,256]{2,1,0:T(8,128)S(1)}, f32[2,128,256]{2,1,0:T(8,128)S(1)}, u32[]{:S(2)}, u32[]{:S(2)}) collective-permute-start(f32[2,128,256]{2,1,0:T(8,128)S(1)} %fusion.14.mine), channel_id=1, source_target_pairs={{0,8},{4,12},{8,0},{12,4},{16,24},{20,28},{24,16},{28,20},{1,9},{5... | collective-permute-start | bytes 786440 | tf_op jit(solution)/shard_map/ppermute | solution.py:350
  85.2 4.3 %shard_map.40 = (bf16[2048,512]{1,0:T(8,128)(2,1)S(1)}, bf16[2048,512]{1,0:T(8,128)(2,1)S(1)}, bf16[256,256]{1,0:T(8,128)(2,1)S(1)}, bf16[256,256]{1,0:T(8,128)(...) custom-call(s32[5]{0:T(128)S(1)} %stack.32.scal, f32[768,128]{1,0:T(8,128)S(1)} %pad_maximum_fusion.q0, ...), custom_call_target="tpu_custom_call" | custom-call | flops 2415919104 | tf_op jit(solution)/shard_map/pallas_call | solution.py:217
  89.5 0.0 collective-permute-done.13.far
  89.6 0.7 collective-permute-start.5
  90.3 4.1 %collective-permute-done.12.near1 = f32[2,128,256]{2,1,0:T(8,128)S(1)} collective-permute-done((f32[2,128,256]{2,1,0:T(8,128)S(1)}, f32[2,128,256]{2,1,0:T(8,128)S(1)}, u32[]{:S(2)}, u32[]{:S(2)}) %collective-permute-start.12) | collective-permute-done | bytes 262176 | tf_op jit(solution)/shard_map/ppermute | solution.py:350
  94.4 1.9 %collective-permute-done.11.near0 = f32[2,128,256]{2,1,0:T(8,128)S(1)} collective-permute-done((f32[2,128,256]{2,1,0:T(8,128)S(1)}, f32[2,128,256]{2,1,0:T(8,128)S(1)}, u32[]{:S(2)}, u32[]{:S(2)}) %collective-permute-start.11) | collective-permute-done | bytes 262176 | tf_op jit(solution)/shard_map/ppermute | solution.py:350
  96.3 6.1 %shard_map.41 = (f32[2048,512]{1,0:T(8,128)S(1)}, f32[512,512]{1,0:T(8,128)S(1)}) custom-call(s32[5]{0:T(128)S(1)} %stack.32.scal, f32[2,128,256]{2,1,0:T(8,128)S(1)} %add.63.mine, f32[2,128,256]{2,1,0:T(8,128)S(1)} %collective-permute-done.11.near0, f32[2,128,256]{2,1,0:T(8,128)S(1)} %collective-permute-done.12.near1, ...), custom_call_target="tpu_custom_call" | custom-call | flops 3221225472 | tf_op jit(solution)/shard_map/pallas_call | solution.py:217
  102.5 0.0 collective-permute-done.5.near0
  102.5 5.4 %shard_map.42 = f32[2048,512]{1,0:T(8,128)} custom-call(s32[5]{0:T(128)S(1)} %stack.32.scal, f32[2,128,256]{2,1,0:T(8,128)S(1)} %fusion.14.mine, f32[2,128,256]{2,1,0:T(8,128)S(1)} %collective-permute-done.5.near0, f32[2,128,256]{2,1,0:T(8,128)S(1)} %collective-permute-done.6.near1, f32[2,128,256]{2,1,0:T(8,128)S(1)} %collective-permute-done.7.far, ...), custom_call_target="tpu_custom_call" | custom-call | flops 3221225472 | tf_op jit(solution)/shard_map/pallas_call | solution.py:217
  (24 shorter events, 0.3 us)
Async XLA Ops:
  9.9 9.3 %collective-permute-start.14 = (f32[2,192,128]{2,1,0:T(8,128)S(1)}, f32[2,192,128]{2,1,0:T(8,128)S(1)}, u32[]{:S(2)}, u32[]{:S(2)}) collective-permute-start(f32[2,192,128]{2,1,0:T(8,128)S(1)} %get-tuple-element.47), channel_id=1, source_target_pairs={{0,4},{4,0},{8,12},{12,8},{16,20},{20,16},{24,28},{28,24},{1,5},{5... | collective-permute-start | bytes 589832 | tf_op jit(solution)/shard_map/ppermute | solution.py:350
  16.9 7.8 %collective-permute-start = (f32[2,128,256]{2,1,0:T(8,128)S(1)}, f32[2,128,256]{2,1,0:T(8,128)S(1)}, u32[]{:S(2)}, u32[]{:S(2)}) collective-permute-start(f32[2,128,256]{2,1,0:T(8,128)S(1)} %get-tuple-element.36), channel_id=1, source_target_pairs={{0,4},{4,0},{8,12},{12,8},{16,20},{20,16},{24,28},{28,24},{1,5},{5... | collective-permute-start | bytes 786440 | tf_op jit(solution)/shard_map/ppermute | solution.py:350
  17.0 25.7 %collective-permute-start.2 = (f32[2,128,256]{2,1,0:T(8,128)S(1)}, f32[2,128,256]{2,1,0:T(8,128)S(1)}, u32[]{:S(2)}, u32[]{:S(2)}) collective-permute-start(f32[2,128,256]{2,1,0:T(8,128)S(1)} %get-tuple-element.39), channel_id=1, source_target_pairs={{0,8},{4,12},{8,0},{12,4},{16,24},{20,28},{24,16},{28,20},{1,9},{5... | collective-permute-start | bytes 786440 | tf_op jit(solution)/shard_map/ppermute | solution.py:350
  19.1 35.9 %collective-permute-start.8 = (f32[2,2,128,256]{3,2,0,1:T(8,128)S(1)}, f32[2,2,128,256]{3,2,0,1:T(8,128)S(1)}, u32[]{:S(2)}, u32[]{:S(2)}) collective-permute-start(f32[2,2,128,256]{3,2,0,1:T(8,128)S(1)} %copy.4), channel_id=1, source_target_pairs={{0,8},{4,12},{8,0},{12,4},{16,24},{20,28},{24,16},{28,20},{1,9},{5... | collective-permute-start | bytes 1572872 | tf_op jit(solution)/shard_map/ppermute | solution.py:350
  19.2 20.3 %collective-permute-start.15 = (f32[192,128]{1,0:T(8,128)S(1)}, f32[192,128]{1,0:T(8,128)S(1)}, u32[]{:S(2)}, u32[]{:S(2)}) collective-permute-start(f32[192,128]{1,0:T(8,128)S(1)} %fusion.11), channel_id=1, source_target_pairs={{0,8},{4,12},{8,0},{12,4},{16,24},{20,28},{24,16},{28,20},{1,9},{5... | collective-permute-start | bytes 294920 | tf_op jit(solution)/shard_map/ppermute | solution.py:350
  24.7 24.0 %collective-permute-start.1 = (f32[128,256]{1,0:T(8,128)S(1)}, f32[128,256]{1,0:T(8,128)S(1)}, u32[]{:S(2)}, u32[]{:S(2)}) collective-permute-start(f32[128,256]{1,0:T(8,128)S(1)} %fusion.7), channel_id=1, source_target_pairs={{0,8},{4,12},{8,0},{12,4},{16,24},{20,28},{24,16},{28,20},{1,9},{5... | collective-permute-start | bytes 393224 | tf_op jit(solution)/shard_map/ppermute | solution.py:350
  39.6 5.7 %collective-permute-start.16 = (f32[192,128]{1,0:T(8,128)S(1)}, f32[192,128]{1,0:T(8,128)S(1)}, u32[]{:S(2)}, u32[]{:S(2)}) collective-permute-start(f32[192,128]{1,0:T(8,128)S(1)} %fusion.13), channel_id=1, source_target_pairs={{0,16},{4,20},{8,24},{12,28},{16,0},{20,4},{24,8},{28,12},{1,17},{... | collective-permute-start | bytes 294920 | tf_op jit(solution)/shard_map/ppermute | solution.py:350
  42.7 13.8 %collective-permute-start.3 = (f32[128,256]{1,0:T(8,128)S(1)}, f32[128,256]{1,0:T(8,128)S(1)}, u32[]{:S(2)}, u32[]{:S(2)}) collective-permute-start(f32[128,256]{1,0:T(8,128)S(1)} %fusion.3), channel_id=1, source_target_pairs={{0,4},{4,0},{8,12},{12,8},{16,20},{20,16},{24,28},{28,24},{1,5},{5... | collective-permute-start | bytes 393224 | tf_op jit(solution)/shard_map/ppermute | solution.py:350
  45.3 5.6 %collective-permute-start.19 = (f32[192,128]{1,0:T(8,128)S(1)}, f32[192,128]{1,0:T(8,128)S(1)}, u32[]{:S(2)}, u32[]{:S(2)}) collective-permute-start(f32[192,128]{1,0:T(8,128)S(1)} %add.67), channel_id=1, source_target_pairs={{0,12},{4,8},{8,4},{12,0},{16,28},{20,24},{24,20},{28,16},{1,13},{... | collective-permute-start | bytes 294920 | tf_op jit(solution)/shard_map/ppermute | solution.py:350
  48.2 4.6 %collective-permute-start.18 = (f32[192,128]{1,0:T(8,128)S(1)}, f32[192,128]{1,0:T(8,128)S(1)}, u32[]{:S(2)}, u32[]{:S(2)}) collective-permute-start(f32[192,128]{1,0:T(8,128)S(1)} %add.67), channel_id=1, source_target_pairs={{0,4},{4,0},{8,12},{12,8},{16,20},{20,16},{24,28},{28,24},{1,5},{5... | collective-permute-start | bytes 294920 | tf_op jit(solution)/shard_map/ppermute | solution.py:350
  48.7 4.6 %collective-permute-start.17 = (f32[192,128]{1,0:T(8,128)S(1)}, f32[192,128]{1,0:T(8,128)S(1)}, u32[]{:S(2)}, u32[]{:S(2)}) collective-permute-start(f32[192,128]{1,0:T(8,128)S(1)} %add.67), channel_id=1, source_target_pairs={{0,8},{4,12},{8,0},{12,4},{16,24},{20,28},{24,16},{28,20},{1,9},{5... | collective-permute-start | bytes 294920 | tf_op jit(solution)/shard_map/ppermute | solution.py:350
  48.9 17.2 %copy-start.1 = (f32[4,256,256]{2,1,0:T(8,128)S(1)}, f32[4,256,256]{2,1,0:T(8,128)}, u32[]{:S(2)}) copy-start(f32[4,256,256]{2,1,0:T(8,128)} %param.5) | copy-start | bytes 3145732
  53.4 12.7 %collective-permute-start.20 = (f32[768,128]{1,0:T(8,128)S(1)}, f32[768,128]{1,0:T(8,128)S(1)}, u32[]{:S(2)}, u32[]{:S(2)}) collective-permute-start(f32[768,128]{1,0:T(8,128)S(1)} %pad_maximum_fusion.q0), channel_id=1, source_target_pairs={{0,2},{1,3},{2,0},{3,1},{4,6},{5,7},{6,4},{7,5},{8,10},{9,11},{10,... | collective-permute-start | bytes 1179656 | tf_op jit(solution)/shard_map/ppermute | solution.py:350
  55.0 6.4 %collective-permute-start.9 = (f32[2,128,256]{2,1,0:T(8,128)S(1)}, f32[2,128,256]{2,1,0:T(8,128)S(1)}, u32[]{:S(2)}, u32[]{:S(2)}) collective-permute-start(f32[2,128,256]{2,1,0:T(8,128)S(1)} %fusion), channel_id=1, source_target_pairs={{0,4},{4,0},{8,12},{12,8},{16,20},{20,16},{24,28},{28,24},{1,5},{5... | collective-permute-start | bytes 786440 | tf_op jit(solution)/shard_map/ppermute | solution.py:350
  56.6 25.0 %collective-permute-start.4 = (f32[2,128,256]{2,1,0:T(8,128)S(1)}, f32[2,128,256]{2,1,0:T(8,128)S(1)}, u32[]{:S(2)}, u32[]{:S(2)}) collective-permute-start(f32[2,128,256]{2,1,0:T(8,128)S(1)} %pad_maximum_fusion.1), channel_id=1, source_target_pairs={{0,16},{4,20},{8,24},{12,28},{16,0},{20,4},{24,8},{28,12},{1,17},{... | collective-permute-start | bytes 786440 | tf_op jit(solution)/shard_map/ppermute | solution.py:350
  61.2 21.0 %collective-permute-start.21 = (f32[768,128]{1,0:T(8,128)S(1)}, f32[768,128]{1,0:T(8,128)S(1)}, u32[]{:S(2)}, u32[]{:S(2)}) collective-permute-start(f32[768,128]{1,0:T(8,128)S(1)} %pad_maximum_fusion.q0), channel_id=1, source_target_pairs={{0,1},{1,0},{2,3},{3,2},{4,5},{5,4},{6,7},{7,6},{8,9},{9,8},{10,11... | collective-permute-start | bytes 1179656 | tf_op jit(solution)/shard_map/ppermute | solution.py:350
  61.5 17.1 %collective-permute-start.10 = (f32[2,128,256]{2,1,0:T(8,128)S(1)}, f32[2,128,256]{2,1,0:T(8,128)S(1)}, u32[]{:S(2)}, u32[]{:S(2)}) collective-permute-start(f32[2,128,256]{2,1,0:T(8,128)S(1)} %fusion.2), channel_id=1, source_target_pairs={{0,16},{4,20},{8,24},{12,28},{16,0},{20,4},{24,8},{28,12},{1,17},{... | collective-permute-start | bytes 786440 | tf_op jit(solution)/shard_map/ppermute | solution.py:350
  66.1 17.1 %collective-permute-start.22 = (f32[768,128]{1,0:T(8,128)S(1)}, f32[768,128]{1,0:T(8,128)S(1)}, u32[]{:S(2)}, u32[]{:S(2)}) collective-permute-start(f32[768,128]{1,0:T(8,128)S(1)} %collective-permute-done.20.q1), channel_id=1, source_target_pairs={{0,1},{1,0},{2,3},{3,2},{4,5},{5,4},{6,7},{7,6},{8,9},{9,8},{10,11... | collective-permute-start | bytes 1179656 | tf_op jit(solution)/shard_map/ppermute | solution.py:350
  78.6 11.0 %collective-permute-start.13 = (f32[2,128,256]{2,1,0:T(8,128)S(1)}, f32[2,128,256]{2,1,0:T(8,128)S(1)}, u32[]{:S(2)}, u32[]{:S(2)}) collective-permute-start(f32[2,128,256]{2,1,0:T(8,128)S(1)} %add.63.mine), channel_id=1, source_target_pairs={{0,12},{4,8},{8,4},{12,0},{16,28},{20,24},{24,20},{28,16},{1,13},{... | collective-permute-start | bytes 786440 | tf_op jit(solution)/shard_map/ppermute | solution.py:350
  79.6 14.8 %collective-permute-start.12 = (f32[2,128,256]{2,1,0:T(8,128)S(1)}, f32[2,128,256]{2,1,0:T(8,128)S(1)}, u32[]{:S(2)}, u32[]{:S(2)}) collective-permute-start(f32[2,128,256]{2,1,0:T(8,128)S(1)} %add.63.mine), channel_id=1, source_target_pairs={{0,8},{4,12},{8,0},{12,4},{16,24},{20,28},{24,16},{28,20},{1,9},{5... | collective-permute-start | bytes 786440 | tf_op jit(solution)/shard_map/ppermute | solution.py:350
  81.6 14.7 %collective-permute-start.11 = (f32[2,128,256]{2,1,0:T(8,128)S(1)}, f32[2,128,256]{2,1,0:T(8,128)S(1)}, u32[]{:S(2)}, u32[]{:S(2)}) collective-permute-start(f32[2,128,256]{2,1,0:T(8,128)S(1)} %add.63.mine), channel_id=1, source_target_pairs={{0,4},{4,0},{8,12},{12,8},{16,20},{20,16},{24,28},{28,24},{1,5},{5... | collective-permute-start | bytes 786440 | tf_op jit(solution)/shard_map/ppermute | solution.py:350
  82.2 20.3 %collective-permute-start.7 = (f32[2,128,256]{2,1,0:T(8,128)S(1)}, f32[2,128,256]{2,1,0:T(8,128)S(1)}, u32[]{:S(2)}, u32[]{:S(2)}) collective-permute-start(f32[2,128,256]{2,1,0:T(8,128)S(1)} %fusion.14.mine), channel_id=1, source_target_pairs={{0,12},{4,8},{8,4},{12,0},{16,28},{20,24},{24,20},{28,16},{1,13},{... | collective-permute-start | bytes 786440 | tf_op jit(solution)/shard_map/ppermute | solution.py:350
  83.2 19.3 %collective-permute-start.6 = (f32[2,128,256]{2,1,0:T(8,128)S(1)}, f32[2,128,256]{2,1,0:T(8,128)S(1)}, u32[]{:S(2)}, u32[]{:S(2)}) collective-permute-start(f32[2,128,256]{2,1,0:T(8,128)S(1)} %fusion.14.mine), channel_id=1, source_target_pairs={{0,8},{4,12},{8,0},{12,4},{16,24},{20,28},{24,16},{28,20},{1,9},{5... | collective-permute-start | bytes 786440 | tf_op jit(solution)/shard_map/ppermute | solution.py:350
  85.2 11.1 %copy-start = (f32[2048,512]{1,0:T(8,128)S(1)}, f32[2048,512]{1,0:T(8,128)}, u32[]{:S(2)}) copy-start(f32[2048,512]{1,0:T(8,128)} %w_ref.1) | copy-start | bytes 12582916
  89.6 13.0 %collective-permute-start.5 = (f32[2,128,256]{2,1,0:T(8,128)S(1)}, f32[2,128,256]{2,1,0:T(8,128)S(1)}, u32[]{:S(2)}, u32[]{:S(2)}) collective-permute-start(f32[2,128,256]{2,1,0:T(8,128)S(1)} %fusion.14.mine), channel_id=1, source_target_pairs={{0,4},{4,0},{8,12},{12,8},{16,20},{20,16},{24,28},{28,24},{1,5},{5... | collective-permute-start | bytes 786440 | tf_op jit(solution)/shard_map/ppermute | solution.py:350
where the time goes:
time: 108 us
  waiting for transfers between devices  40.8 us (38%)
  starting transfers between devices  36.8 us (34%)
  Pallas kernels  29.7 us (28%)
    ppermute x23, waiting for transfers between devices, swap(): return lax.ppermute(value, axis, [(i, i ^ flip) for i in range(size)])  40.8 us
    ppermute x23, starting transfers between devices, swap(): return lax.ppermute(value, axis, [(i, i ^ flip) for i in range(size)])  36.8 us
    pallas_call x6, Pallas kernels, call(): pl.pallas_call(kernel, in_specs=[pl.BlockSpec(memory_space=pltpu.SMEM)] +...  29.7 us
  transfers between devices with their start and end apart: 23, of which 10 were waited for; matrix products, arithmetic and copies ran while one was open for 0% of the time, Pallas kernels for 13%

commit v1 on v0

--- a/solution.py
+++ b/solution.py
@@ -9,7 +9,7 @@
 
 
 RB = 64
-TILES = 8
+TILES = 4
 
 
 def split(value):
@@ -69,13 +69,15 @@
 
     early = [[fetch(k, t) for k in range(-1, count)] for t in range(TILES)]
     late = [[fetch(k, t) for k in range(count, panels)] for t in range(TILES)]
-    for copies in early + late:
+    for copies in early:
         for copy in copies:
             copy.start()
     for t in range(TILES):
         r = rows_of(t, rows)
         for copy in early[t]:
             copy.wait()
+        for copy in late[t]:
+            copy.start()
         left = split(wbuf[r, :].T)
         wh[:, r], wl[:, r] = left
         for k in range(count):

time: 108 us -> 109 us (level)
  transfers between devices with their start and end apart: 23 -> 23, of which waited for: 10 -> 10; matrix products, arithmetic and copies ran while one was open for 0% -> 0% of each run, Pallas kernels for 13% -> 14%
where the time goes in v1:
time: 109 us
  waiting for transfers between devices  40.8 us (37%)
  starting transfers between devices  36.8 us (34%)
  Pallas kernels  30 us (28%)
    ppermute x23, waiting for transfers between devices, swap(): return lax.ppermute(value, axis, [(i, i ^ flip) for i in range(size)])  40.8 us
    ppermute x23, starting transfers between devices, swap(): return lax.ppermute(value, axis, [(i, i ^ flip) for i in range(size)])  36.8 us
    pallas_call x6, Pallas kernels, call(): pl.pallas_call(kernel, in_specs=[pl.BlockSpec(memory_space=pltpu.SMEM)] +...  30 us
  transfers between devices with their start and end apart: 23, of which 10 were waited for; matrix products, arithmetic and copies ran while one was open for 0% of the time, Pallas kernels for 14%

profile of v1, /device:TPU:0, one launch (start us, length us, event | category | flops | bytes accessed | tf_op | source)
XLA Modules:
  0.0 108.5 jit_solution(7982847973612620061)
XLA Ops:
  0.0 0.1 stack.32.scal
  0.1 7.3 %shard_map.37 = (f32[2,128,256]{2,1,0:T(8,128)S(1)}, f32[2,128,256]{2,1,0:T(8,128)S(1)}, f32[2,2,128,256]{3,2,1,0:T(8,128)S(1)}, bf16[512,2048]{1,0:T(8,128)(2,1...) custom-call(s32[5]{0:T(128)S(1)} %stack.32.scal, ...), custom_call_target="tpu_custom_call" | custom-call | flops 3221225472 | tf_op jit(solution)/shard_map/pallas_call | solution.py:219
  7.4 2.4 %shard_map.39 = (f32[192,128]{1,0:T(8,128)S(1)}, f32[192,128]{1,0:T(8,128)S(1)}, f32[2,192,128]{2,1,0:T(8,128)S(1)}) custom-call(s32[5]{0:T(128)S(1)} %stack.32.scal, bf16[2048,512]{1,0:T(8,128)(2,1)S(1)} %get-tuple-element.44.eh.vh, bf16[2048,512]{1,0:T(8,128)(2,1)S(1)} %get-tuple-element.45.el.vl, bf16[2048,512]{1,0:T(8,128)(2,1)S(1)} %get-tuple-element.33.vh.lh, ...), custom_call_target="tpu_custom_call" | custom-call | flops 1207959552 | tf_op jit(solution)/shard_map/pallas_call | solution.py:219
  9.8 3.0 %collective-permute-start.14 = (f32[2,192,128]{2,1,0:T(8,128)S(1)}, f32[2,192,128]{2,1,0:T(8,128)S(1)}, u32[]{:S(2)}, u32[]{:S(2)}) collective-permute-start(f32[2,192,128]{2,1,0:T(8,128)S(1)} %get-tuple-element.47), channel_id=1, source_target_pairs={{0,4},{4,0},{8,12},{12,8},{16,20},{20,16},{24,28},{28,24},{1,5},{5... | collective-permute-start | bytes 589832 | tf_op jit(solution)/shard_map/ppermute | solution.py:352
  12.8 3.9 %shard_map.38 = (f32[128,256]{1,0:T(8,128)S(1)}, f32[128,256]{1,0:T(8,128)S(1)}, f32[2,128,256]{2,1,0:T(8,128)S(1)}, f32[128,256]{1,0:T(8,128)S(1)}, f32[128,256]{1,0:T(8,128)S(1)}, /*index=5*/f32[2,128,256]{2,1,0:T(8,128)S(1)}) custom-call(s32[5]{0:T(128)S(1)} %stack.32.scal, bf16[512,2048]{1,0:T(8,128)(2,1)S(1)} %get-tuple-element.31.wh, ...), custom_call_target="tpu_custom_call" | custom-call | flops 3221225472 | tf_op jit(solution)/shard_map/pallas_call | solution.py:219
  16.8 0.1 collective-permute-start
  16.9 2.1 %collective-permute-start.2 = (f32[2,128,256]{2,1,0:T(8,128)S(1)}, f32[2,128,256]{2,1,0:T(8,128)S(1)}, u32[]{:S(2)}, u32[]{:S(2)}) collective-permute-start(f32[2,128,256]{2,1,0:T(8,128)S(1)} %get-tuple-element.39), channel_id=1, source_target_pairs={{0,8},{4,12},{8,0},{12,4},{16,24},{20,28},{24,16},{28,20},{1,9},{5... | collective-permute-start | bytes 786440 | tf_op jit(solution)/shard_map/ppermute | solution.py:352
  19.0 0.1 collective-permute-start.8
  19.1 0.0 collective-permute-done.14
  19.1 2.1 %collective-permute-start.15 = (f32[192,128]{1,0:T(8,128)S(1)}, f32[192,128]{1,0:T(8,128)S(1)}, u32[]{:S(2)}, u32[]{:S(2)}) collective-permute-start(f32[192,128]{1,0:T(8,128)S(1)} %fusion.11), channel_id=1, source_target_pairs={{0,8},{4,12},{8,0},{12,4},{16,24},{20,28},{24,16},{28,20},{1,9},{5... | collective-permute-start | bytes 294920 | tf_op jit(solution)/shard_map/ppermute | solution.py:352
  21.2 3.4 %collective-permute-done = f32[2,128,256]{2,1,0:T(8,128)S(1)} collective-permute-done((f32[2,128,256]{2,1,0:T(8,128)S(1)}, f32[2,128,256]{2,1,0:T(8,128)S(1)}, u32[]{:S(2)}, u32[]{:S(2)}) %collective-permute-start) | collective-permute-done | bytes 262176 | tf_op jit(solution)/shard_map/ppermute | solution.py:352
  24.6 1.6 %collective-permute-start.1 = (f32[128,256]{1,0:T(8,128)S(1)}, f32[128,256]{1,0:T(8,128)S(1)}, u32[]{:S(2)}, u32[]{:S(2)}) collective-permute-start(f32[128,256]{1,0:T(8,128)S(1)} %fusion.7), channel_id=1, source_target_pairs={{0,8},{4,12},{8,0},{12,4},{16,24},{20,28},{24,16},{28,20},{1,9},{5... | collective-permute-start | bytes 393224 | tf_op jit(solution)/shard_map/ppermute | solution.py:352
  26.3 13.2 %collective-permute-done.15 = f32[192,128]{1,0:T(8,128)S(1)} collective-permute-done((f32[192,128]{1,0:T(8,128)S(1)}, f32[192,128]{1,0:T(8,128)S(1)}, u32[]{:S(2)}, u32[]{:S(2)}) %collective-permute-start.15) | collective-permute-done | bytes 98336 | tf_op jit(solution)/shard_map/ppermute | solution.py:352
  39.5 3.1 %collective-permute-start.16 = (f32[192,128]{1,0:T(8,128)S(1)}, f32[192,128]{1,0:T(8,128)S(1)}, u32[]{:S(2)}, u32[]{:S(2)}) collective-permute-start(f32[192,128]{1,0:T(8,128)S(1)} %fusion.13), channel_id=1, source_target_pairs={{0,16},{4,20},{8,24},{12,28},{16,0},{20,4},{24,8},{28,12},{1,17},{... | collective-permute-start | bytes 294920 | tf_op jit(solution)/shard_map/ppermute | solution.py:352
  42.6 0.0 collective-permute-done.2
  42.6 1.6 %collective-permute-start.3 = (f32[128,256]{1,0:T(8,128)S(1)}, f32[128,256]{1,0:T(8,128)S(1)}, u32[]{:S(2)}, u32[]{:S(2)}) collective-permute-start(f32[128,256]{1,0:T(8,128)S(1)} %fusion.3), channel_id=1, source_target_pairs={{0,4},{4,0},{8,12},{12,8},{16,20},{20,16},{24,28},{28,24},{1,5},{5... | collective-permute-start | bytes 393224 | tf_op jit(solution)/shard_map/ppermute | solution.py:352
  44.2 1.0 collective-permute-done.16
  45.2 2.9 %collective-permute-start.19 = (f32[192,128]{1,0:T(8,128)S(1)}, f32[192,128]{1,0:T(8,128)S(1)}, u32[]{:S(2)}, u32[]{:S(2)}) collective-permute-start(f32[192,128]{1,0:T(8,128)S(1)} %add.67), channel_id=1, source_target_pairs={{0,12},{4,8},{8,4},{12,0},{16,28},{20,24},{24,20},{28,16},{1,13},{... | collective-permute-start | bytes 294920 | tf_op jit(solution)/shard_map/ppermute | solution.py:352
  48.1 0.5 collective-permute-start.18
  48.6 0.0 collective-permute-done.1
  48.6 0.2 collective-permute-start.17
  48.8 2.0 %collective-permute-done.19 = f32[192,128]{1,0:T(8,128)S(1)} collective-permute-done((f32[192,128]{1,0:T(8,128)S(1)}, f32[192,128]{1,0:T(8,128)S(1)}, u32[]{:S(2)}, u32[]{:S(2)}) %collective-permute-start.19) | collective-permute-done | bytes 98336 | tf_op jit(solution)/shard_map/ppermute | solution.py:352
  50.8 1.9 %collective-permute-done.18 = f32[192,128]{1,0:T(8,128)S(1)} collective-permute-done((f32[192,128]{1,0:T(8,128)S(1)}, f32[192,128]{1,0:T(8,128)S(1)}, u32[]{:S(2)}, u32[]{:S(2)}) %collective-permute-start.18) | collective-permute-done | bytes 98336 | tf_op jit(solution)/shard_map/ppermute | solution.py:352
  52.7 0.5 collective-permute-done.17
  53.3 1.6 %collective-permute-start.20 = (f32[768,128]{1,0:T(8,128)S(1)}, f32[768,128]{1,0:T(8,128)S(1)}, u32[]{:S(2)}, u32[]{:S(2)}) collective-permute-start(f32[768,128]{1,0:T(8,128)S(1)} %pad_maximum_fusion.q0), channel_id=1, source_target_pairs={{0,2},{1,3},{2,0},{3,1},{4,6},{5,7},{6,4},{7,5},{8,10},{9,11},{10,... | collective-permute-start | bytes 1179656 | tf_op jit(solution)/shard_map/ppermute | solution.py:352
  54.9 1.6 %collective-permute-start.9 = (f32[2,128,256]{2,1,0:T(8,128)S(1)}, f32[2,128,256]{2,1,0:T(8,128)S(1)}, u32[]{:S(2)}, u32[]{:S(2)}) collective-permute-start(f32[2,128,256]{2,1,0:T(8,128)S(1)} %fusion), channel_id=1, source_target_pairs={{0,4},{4,0},{8,12},{12,8},{16,20},{20,16},{24,28},{28,24},{1,5},{5... | collective-permute-start | bytes 786440 | tf_op jit(solution)/shard_map/ppermute | solution.py:352
  56.5 4.6 %collective-permute-start.4 = (f32[2,128,256]{2,1,0:T(8,128)S(1)}, f32[2,128,256]{2,1,0:T(8,128)S(1)}, u32[]{:S(2)}, u32[]{:S(2)}) collective-permute-start(f32[2,128,256]{2,1,0:T(8,128)S(1)} %pad_maximum_fusion.1), channel_id=1, source_target_pairs={{0,16},{4,20},{8,24},{12,28},{16,0},{20,4},{24,8},{28,12},{1,17},{... | collective-permute-start | bytes 786440 | tf_op jit(solution)/shard_map/ppermute | solution.py:352
  61.1 0.2 collective-permute-done.9
  61.3 0.1 fusion.2
  61.4 4.6 %collective-permute-start.10 = (f32[2,128,256]{2,1,0:T(8,128)S(1)}, f32[2,128,256]{2,1,0:T(8,128)S(1)}, u32[]{:S(2)}, u32[]{:S(2)}) collective-permute-start(f32[2,128,256]{2,1,0:T(8,128)S(1)} %fusion.2), channel_id=1, source_target_pairs={{0,16},{4,20},{8,24},{12,28},{16,0},{20,4},{24,8},{28,12},{1,17},{... | collective-permute-start | bytes 786440 | tf_op jit(solution)/shard_map/ppermute | solution.py:352
  66.0 0.0 collective-permute-done.20.q1
  66.0 0.0 collective-permute-start.22
  66.0 0.1 fusion.15
  66.1 12.4 %collective-permute-done.10 = f32[2,128,256]{2,1,0:T(8,128)S(1)} collective-permute-done((f32[2,128,256]{2,1,0:T(8,128)S(1)}, f32[2,128,256]{2,1,0:T(8,128)S(1)}, u32[]{:S(2)}, u32[]{:S(2)}) %collective-permute-start.10) | collective-permute-done | bytes 262176 | tf_op jit(solution)/shard_map/ppermute | solution.py:352
  78.5 1.0 collective-permute-start.13
  79.5 2.0 %collective-permute-start.12 = (f32[2,128,256]{2,1,0:T(8,128)S(1)}, f32[2,128,256]{2,1,0:T(8,128)S(1)}, u32[]{:S(2)}, u32[]{:S(2)}) collective-permute-start(f32[2,128,256]{2,1,0:T(8,128)S(1)} %add.63.mine), channel_id=1, source_target_pairs={{0,8},{4,12},{8,0},{12,4},{16,24},{20,28},{24,16},{28,20},{1,9},{5... | collective-permute-start | bytes 786440 | tf_op jit(solution)/shard_map/ppermute | solution.py:352
  81.5 0.6 collective-permute-start.11
  82.1 1.0 collective-permute-start.7
  83.1 0.0 collective-permute-done.22.q3
  83.1 2.0 %collective-permute-start.6 = (f32[2,128,256]{2,1,0:T(8,128)S(1)}, f32[2,128,256]{2,1,0:T(8,128)S(1)}, u32[]{:S(2)}, u32[]{:S(2)}) collective-permute-start(f32[2,128,256]{2,1,0:T(8,128)S(1)} %fusion.14.mine), channel_id=1, source_target_pairs={{0,8},{4,12},{8,0},{12,4},{16,24},{20,28},{24,16},{28,20},{1,9},{5... | collective-permute-start | bytes 786440 | tf_op jit(solution)/shard_map/ppermute | solution.py:352
  85.1 4.3 %shard_map.40 = (bf16[2048,512]{1,0:T(8,128)(2,1)S(1)}, bf16[2048,512]{1,0:T(8,128)(2,1)S(1)}, bf16[256,256]{1,0:T(8,128)(2,1)S(1)}, bf16[256,256]{1,0:T(8,128)(...) custom-call(s32[5]{0:T(128)S(1)} %stack.32.scal, f32[768,128]{1,0:T(8,128)S(1)} %pad_maximum_fusion.q0, ...), custom_call_target="tpu_custom_call" | custom-call | flops 2415919104 | tf_op jit(solution)/shard_map/pallas_call | solution.py:219
  89.4 0.8 collective-permute-start.5
  90.2 4.1 %collective-permute-done.12.near1 = f32[2,128,256]{2,1,0:T(8,128)S(1)} collective-permute-done((f32[2,128,256]{2,1,0:T(8,128)S(1)}, f32[2,128,256]{2,1,0:T(8,128)S(1)}, u32[]{:S(2)}, u32[]{:S(2)}) %collective-permute-start.12) | collective-permute-done | bytes 262176 | tf_op jit(solution)/shard_map/ppermute | solution.py:352
  94.3 1.9 %collective-permute-done.11.near0 = f32[2,128,256]{2,1,0:T(8,128)S(1)} collective-permute-done((f32[2,128,256]{2,1,0:T(8,128)S(1)}, f32[2,128,256]{2,1,0:T(8,128)S(1)}, u32[]{:S(2)}, u32[]{:S(2)}) %collective-permute-start.11) | collective-permute-done | bytes 262176 | tf_op jit(solution)/shard_map/ppermute | solution.py:352
  96.2 6.8 %shard_map.41 = (f32[2048,512]{1,0:T(8,128)S(1)}, f32[512,512]{1,0:T(8,128)S(1)}) custom-call(s32[5]{0:T(128)S(1)} %stack.32.scal, f32[2,128,256]{2,1,0:T(8,128)S(1)} %add.63.mine, f32[2,128,256]{2,1,0:T(8,128)S(1)} %collective-permute-done.11.near0, f32[2,128,256]{2,1,0:T(8,128)S(1)} %collective-permute-done.12.near1, ...), custom_call_target="tpu_custom_call" | custom-call | flops 3221225472 | tf_op jit(solution)/shard_map/pallas_call | solution.py:219
  103.0 0.0 collective-permute-done.7.far
  103.0 0.0 collective-permute-done.6.near1
  103.0 5.3 %shard_map.42 = f32[2048,512]{1,0:T(8,128)} custom-call(s32[5]{0:T(128)S(1)} %stack.32.scal, f32[2,128,256]{2,1,0:T(8,128)S(1)} %fusion.14.mine, f32[2,128,256]{2,1,0:T(8,128)S(1)} %collective-permute-done.5.near0, f32[2,128,256]{2,1,0:T(8,128)S(1)} %collective-permute-done.6.near1, f32[2,128,256]{2,1,0:T(8,128)S(1)} %collective-permute-done.7.far, ...), custom_call_target="tpu_custom_call" | custom-call | flops 3221225472 | tf_op jit(solution)/shard_map/pallas_call | solution.py:219
  (24 shorter events, 0.3 us)
Async XLA Ops:
  9.8 9.3 %collective-permute-start.14 = (f32[2,192,128]{2,1,0:T(8,128)S(1)}, f32[2,192,128]{2,1,0:T(8,128)S(1)}, u32[]{:S(2)}, u32[]{:S(2)}) collective-permute-start(f32[2,192,128]{2,1,0:T(8,128)S(1)} %get-tuple-element.47), channel_id=1, source_target_pairs={{0,4},{4,0},{8,12},{12,8},{16,20},{20,16},{24,28},{28,24},{1,5},{5... | collective-permute-start | bytes 589832 | tf_op jit(solution)/shard_map/ppermute | solution.py:352
  16.8 7.8 %collective-permute-start = (f32[2,128,256]{2,1,0:T(8,128)S(1)}, f32[2,128,256]{2,1,0:T(8,128)S(1)}, u32[]{:S(2)}, u32[]{:S(2)}) collective-permute-start(f32[2,128,256]{2,1,0:T(8,128)S(1)} %get-tuple-element.36), channel_id=1, source_target_pairs={{0,4},{4,0},{8,12},{12,8},{16,20},{20,16},{24,28},{28,24},{1,5},{5... | collective-permute-start | bytes 786440 | tf_op jit(solution)/shard_map/ppermute | solution.py:352
  16.9 25.7 %collective-permute-start.2 = (f32[2,128,256]{2,1,0:T(8,128)S(1)}, f32[2,128,256]{2,1,0:T(8,128)S(1)}, u32[]{:S(2)}, u32[]{:S(2)}) collective-permute-start(f32[2,128,256]{2,1,0:T(8,128)S(1)} %get-tuple-element.39), channel_id=1, source_target_pairs={{0,8},{4,12},{8,0},{12,4},{16,24},{20,28},{24,16},{28,20},{1,9},{5... | collective-permute-start | bytes 786440 | tf_op jit(solution)/shard_map/ppermute | solution.py:352
  19.0 35.8 %collective-permute-start.8 = (f32[2,2,128,256]{3,2,0,1:T(8,128)S(1)}, f32[2,2,128,256]{3,2,0,1:T(8,128)S(1)}, u32[]{:S(2)}, u32[]{:S(2)}) collective-permute-start(f32[2,2,128,256]{3,2,0,1:T(8,128)S(1)} %copy.4), channel_id=1, source_target_pairs={{0,8},{4,12},{8,0},{12,4},{16,24},{20,28},{24,16},{28,20},{1,9},{5... | collective-permute-start | bytes 1572872 | tf_op jit(solution)/shard_map/ppermute | solution.py:352
  19.1 20.3 %collective-permute-start.15 = (f32[192,128]{1,0:T(8,128)S(1)}, f32[192,128]{1,0:T(8,128)S(1)}, u32[]{:S(2)}, u32[]{:S(2)}) collective-permute-start(f32[192,128]{1,0:T(8,128)S(1)} %fusion.11), channel_id=1, source_target_pairs={{0,8},{4,12},{8,0},{12,4},{16,24},{20,28},{24,16},{28,20},{1,9},{5... | collective-permute-start | bytes 294920 | tf_op jit(solution)/shard_map/ppermute | solution.py:352
  24.6 24.0 %collective-permute-start.1 = (f32[128,256]{1,0:T(8,128)S(1)}, f32[128,256]{1,0:T(8,128)S(1)}, u32[]{:S(2)}, u32[]{:S(2)}) collective-permute-start(f32[128,256]{1,0:T(8,128)S(1)} %fusion.7), channel_id=1, source_target_pairs={{0,8},{4,12},{8,0},{12,4},{16,24},{20,28},{24,16},{28,20},{1,9},{5... | collective-permute-start | bytes 393224 | tf_op jit(solution)/shard_map/ppermute | solution.py:352
  39.5 5.7 %collective-permute-start.16 = (f32[192,128]{1,0:T(8,128)S(1)}, f32[192,128]{1,0:T(8,128)S(1)}, u32[]{:S(2)}, u32[]{:S(2)}) collective-permute-start(f32[192,128]{1,0:T(8,128)S(1)} %fusion.13), channel_id=1, source_target_pairs={{0,16},{4,20},{8,24},{12,28},{16,0},{20,4},{24,8},{28,12},{1,17},{... | collective-permute-start | bytes 294920 | tf_op jit(solution)/shard_map/ppermute | solution.py:352
  42.6 13.9 %collective-permute-start.3 = (f32[128,256]{1,0:T(8,128)S(1)}, f32[128,256]{1,0:T(8,128)S(1)}, u32[]{:S(2)}, u32[]{:S(2)}) collective-permute-start(f32[128,256]{1,0:T(8,128)S(1)} %fusion.3), channel_id=1, source_target_pairs={{0,4},{4,0},{8,12},{12,8},{16,20},{20,16},{24,28},{28,24},{1,5},{5... | collective-permute-start | bytes 393224 | tf_op jit(solution)/shard_map/ppermute | solution.py:352
  45.2 5.6 %collective-permute-start.19 = (f32[192,128]{1,0:T(8,128)S(1)}, f32[192,128]{1,0:T(8,128)S(1)}, u32[]{:S(2)}, u32[]{:S(2)}) collective-permute-start(f32[192,128]{1,0:T(8,128)S(1)} %add.67), channel_id=1, source_target_pairs={{0,12},{4,8},{8,4},{12,0},{16,28},{20,24},{24,20},{28,16},{1,13},{... | collective-permute-start | bytes 294920 | tf_op jit(solution)/shard_map/ppermute | solution.py:352
  48.1 4.6 %collective-permute-start.18 = (f32[192,128]{1,0:T(8,128)S(1)}, f32[192,128]{1,0:T(8,128)S(1)}, u32[]{:S(2)}, u32[]{:S(2)}) collective-permute-start(f32[192,128]{1,0:T(8,128)S(1)} %add.67), channel_id=1, source_target_pairs={{0,4},{4,0},{8,12},{12,8},{16,20},{20,16},{24,28},{28,24},{1,5},{5... | collective-permute-start | bytes 294920 | tf_op jit(solution)/shard_map/ppermute | solution.py:352
  48.6 4.6 %collective-permute-start.17 = (f32[192,128]{1,0:T(8,128)S(1)}, f32[192,128]{1,0:T(8,128)S(1)}, u32[]{:S(2)}, u32[]{:S(2)}) collective-permute-start(f32[192,128]{1,0:T(8,128)S(1)} %add.67), channel_id=1, source_target_pairs={{0,8},{4,12},{8,0},{12,4},{16,24},{20,28},{24,16},{28,20},{1,9},{5... | collective-permute-start | bytes 294920 | tf_op jit(solution)/shard_map/ppermute | solution.py:352
  48.8 17.2 %copy-start.1 = (f32[4,256,256]{2,1,0:T(8,128)S(1)}, f32[4,256,256]{2,1,0:T(8,128)}, u32[]{:S(2)}) copy-start(f32[4,256,256]{2,1,0:T(8,128)} %param.5) | copy-start | bytes 3145732
  53.3 12.7 %collective-permute-start.20 = (f32[768,128]{1,0:T(8,128)S(1)}, f32[768,128]{1,0:T(8,128)S(1)}, u32[]{:S(2)}, u32[]{:S(2)}) collective-permute-start(f32[768,128]{1,0:T(8,128)S(1)} %pad_maximum_fusion.q0), channel_id=1, source_target_pairs={{0,2},{1,3},{2,0},{3,1},{4,6},{5,7},{6,4},{7,5},{8,10},{9,11},{10,... | collective-permute-start | bytes 1179656 | tf_op jit(solution)/shard_map/ppermute | solution.py:352
  54.9 6.4 %collective-permute-start.9 = (f32[2,128,256]{2,1,0:T(8,128)S(1)}, f32[2,128,256]{2,1,0:T(8,128)S(1)}, u32[]{:S(2)}, u32[]{:S(2)}) collective-permute-start(f32[2,128,256]{2,1,0:T(8,128)S(1)} %fusion), channel_id=1, source_target_pairs={{0,4},{4,0},{8,12},{12,8},{16,20},{20,16},{24,28},{28,24},{1,5},{5... | collective-permute-start | bytes 786440 | tf_op jit(solution)/shard_map/ppermute | solution.py:352
  56.5 25.0 %collective-permute-start.4 = (f32[2,128,256]{2,1,0:T(8,128)S(1)}, f32[2,128,256]{2,1,0:T(8,128)S(1)}, u32[]{:S(2)}, u32[]{:S(2)}) collective-permute-start(f32[2,128,256]{2,1,0:T(8,128)S(1)} %pad_maximum_fusion.1), channel_id=1, source_target_pairs={{0,16},{4,20},{8,24},{12,28},{16,0},{20,4},{24,8},{28,12},{1,17},{... | collective-permute-start | bytes 786440 | tf_op jit(solution)/shard_map/ppermute | solution.py:352
  61.1 21.0 %collective-permute-start.21 = (f32[768,128]{1,0:T(8,128)S(1)}, f32[768,128]{1,0:T(8,128)S(1)}, u32[]{:S(2)}, u32[]{:S(2)}) collective-permute-start(f32[768,128]{1,0:T(8,128)S(1)} %pad_maximum_fusion.q0), channel_id=1, source_target_pairs={{0,1},{1,0},{2,3},{3,2},{4,5},{5,4},{6,7},{7,6},{8,9},{9,8},{10,11... | collective-permute-start | bytes 1179656 | tf_op jit(solution)/shard_map/ppermute | solution.py:352
  61.4 17.1 %collective-permute-start.10 = (f32[2,128,256]{2,1,0:T(8,128)S(1)}, f32[2,128,256]{2,1,0:T(8,128)S(1)}, u32[]{:S(2)}, u32[]{:S(2)}) collective-permute-start(f32[2,128,256]{2,1,0:T(8,128)S(1)} %fusion.2), channel_id=1, source_target_pairs={{0,16},{4,20},{8,24},{12,28},{16,0},{20,4},{24,8},{28,12},{1,17},{... | collective-permute-start | bytes 786440 | tf_op jit(solution)/shard_map/ppermute | solution.py:352
  66.0 17.2 %collective-permute-start.22 = (f32[768,128]{1,0:T(8,128)S(1)}, f32[768,128]{1,0:T(8,128)S(1)}, u32[]{:S(2)}, u32[]{:S(2)}) collective-permute-start(f32[768,128]{1,0:T(8,128)S(1)} %collective-permute-done.20.q1), channel_id=1, source_target_pairs={{0,1},{1,0},{2,3},{3,2},{4,5},{5,4},{6,7},{7,6},{8,9},{9,8},{10,11... | collective-permute-start | bytes 1179656 | tf_op jit(solution)/shard_map/ppermute | solution.py:352
  78.5 10.9 %collective-permute-start.13 = (f32[2,128,256]{2,1,0:T(8,128)S(1)}, f32[2,128,256]{2,1,0:T(8,128)S(1)}, u32[]{:S(2)}, u32[]{:S(2)}) collective-permute-start(f32[2,128,256]{2,1,0:T(8,128)S(1)} %add.63.mine), channel_id=1, source_target_pairs={{0,12},{4,8},{8,4},{12,0},{16,28},{20,24},{24,20},{28,16},{1,13},{... | collective-permute-start | bytes 786440 | tf_op jit(solution)/shard_map/ppermute | solution.py:352
  79.5 14.8 %collective-permute-start.12 = (f32[2,128,256]{2,1,0:T(8,128)S(1)}, f32[2,128,256]{2,1,0:T(8,128)S(1)}, u32[]{:S(2)}, u32[]{:S(2)}) collective-permute-start(f32[2,128,256]{2,1,0:T(8,128)S(1)} %add.63.mine), channel_id=1, source_target_pairs={{0,8},{4,12},{8,0},{12,4},{16,24},{20,28},{24,16},{28,20},{1,9},{5... | collective-permute-start | bytes 786440 | tf_op jit(solution)/shard_map/ppermute | solution.py:352
  81.5 14.7 %collective-permute-start.11 = (f32[2,128,256]{2,1,0:T(8,128)S(1)}, f32[2,128,256]{2,1,0:T(8,128)S(1)}, u32[]{:S(2)}, u32[]{:S(2)}) collective-permute-start(f32[2,128,256]{2,1,0:T(8,128)S(1)} %add.63.mine), channel_id=1, source_target_pairs={{0,4},{4,0},{8,12},{12,8},{16,20},{20,16},{24,28},{28,24},{1,5},{5... | collective-permute-start | bytes 786440 | tf_op jit(solution)/shard_map/ppermute | solution.py:352
  82.1 20.9 %collective-permute-start.7 = (f32[2,128,256]{2,1,0:T(8,128)S(1)}, f32[2,128,256]{2,1,0:T(8,128)S(1)}, u32[]{:S(2)}, u32[]{:S(2)}) collective-permute-start(f32[2,128,256]{2,1,0:T(8,128)S(1)} %fusion.14.mine), channel_id=1, source_target_pairs={{0,12},{4,8},{8,4},{12,0},{16,28},{20,24},{24,20},{28,16},{1,13},{... | collective-permute-start | bytes 786440 | tf_op jit(solution)/shard_map/ppermute | solution.py:352
  83.1 19.9 %collective-permute-start.6 = (f32[2,128,256]{2,1,0:T(8,128)S(1)}, f32[2,128,256]{2,1,0:T(8,128)S(1)}, u32[]{:S(2)}, u32[]{:S(2)}) collective-permute-start(f32[2,128,256]{2,1,0:T(8,128)S(1)} %fusion.14.mine), channel_id=1, source_target_pairs={{0,8},{4,12},{8,0},{12,4},{16,24},{20,28},{24,16},{28,20},{1,9},{5... | collective-permute-start | bytes 786440 | tf_op jit(solution)/shard_map/ppermute | solution.py:352
  85.1 11.1 %copy-start = (f32[2048,512]{1,0:T(8,128)S(1)}, f32[2048,512]{1,0:T(8,128)}, u32[]{:S(2)}) copy-start(f32[2048,512]{1,0:T(8,128)} %w_ref.1) | copy-start | bytes 12582916
  89.4 13.6 %collective-permute-start.5 = (f32[2,128,256]{2,1,0:T(8,128)S(1)}, f32[2,128,256]{2,1,0:T(8,128)S(1)}, u32[]{:S(2)}, u32[]{:S(2)}) collective-permute-start(f32[2,128,256]{2,1,0:T(8,128)S(1)} %fusion.14.mine), channel_id=1, source_target_pairs={{0,4},{4,0},{8,12},{12,8},{16,20},{20,16},{24,28},{28,24},{1,5},{5... | collective-permute-start | bytes 786440 | tf_op jit(solution)/shard_map/ppermute | solution.py:352
